TPU v7x, 128 devices: a whole 4x4x4 slice. The times are simulated.
128 devices in a mesh: sx: 8 (over y, core), sy: 16 (over x, z).
Axes of the slice: x: 4, y: 4, z: 4, core: 2. Of those that a mesh axis runs over, the one named last changes fastest.
Arguments:
- loads: float32 [8, 16, 1536, 256], P('sx', 'sy')
- schur_flex: float32 [8, 16, 1536, 1536], P('sx', 'sy'), as said below
- dirichlet: float32 [8, 16, 1536, 1536], P('sx', 'sy'), as said below
- coupling: float32 [8, 16, 16, 1536], P('sx', 'sy'), may hold values from -0.3125 to 0.3125
- corner_index: int32 [8, 16, 16], P('sx', 'sy'), may hold values from 0 to 512, as said below
- face_lists: int32 [8, 16, 4, 384], P('sx', 'sy'), may hold values from 0 to 383, as said below
- coarse_inverse: float32 [512, 512], P(('sx', 'sy')), as said below
Outputs:
- multipliers: float32 [8, 16, 1536, 256], P('sx', 'sy')
- residual: float32 [8, 16, 1536, 256], P('sx', 'sy')
Inputs may be any that keep to these rules, and one draw needn't show every extreme that they name: `corner_index`: each subdomain lists 4 coarse dofs for each of its four corners; 512 marks a corner on the clamped edges of the panel, which has no coarse dof; every coarse dof below 512 is named by some subdomain. `face_lists`: each face's list is a permutation of the 384 dofs of the facing face; the facing lists of two neighbouring subdomains are inverse permutations. `schur_flex`: symmetric positive definite for every subdomain. `dirichlet`: symmetric positive definite for every subdomain. `coarse_inverse`: symmetric positive definite.
All inputs are finite; a program needn't handle non-finite values.
Results may differ from a plain program's by a relative error of at most 0.00017.
Values sent between devices are 32-bit elements; how exact they have to be, the bound alone decides.
A program may use at most 128 MiB of HBM per device.

v0:
```python
import jax
import jax.numpy as jnp
from jax import lax
from jax.sharding import PartitionSpec as P

ITERS = 2


def shifted(block, axis, distance):
    devices = range(lax.axis_size(axis))
    route = [(i - distance, i) for i in devices if i - distance in devices]
    return lax.ppermute(block, axis, route)


def jump(field, face_index):
    size = field.shape[0] // 4
    width = field.shape[1]
    face_rows = field.reshape(4, size, width)
    from_low_x = shifted(face_rows[1], "sx", 1)
    from_high_x = shifted(face_rows[0], "sx", -1)
    from_low_y = shifted(face_rows[3], "sy", 1)
    from_high_y = shifted(face_rows[2], "sy", -1)
    received = jnp.stack([from_low_x, from_high_x, from_low_y, from_high_y], axis=0)
    matched = received[jnp.arange(4, dtype=jnp.int32)[:, None], face_index]
    return (face_rows - matched).reshape(4 * size, width)


def coarse_solve(coarse_rhs, stiffness_inverse_lines):
    highest = lax.Precision.HIGHEST
    total = lax.psum(coarse_rhs, ("sx", "sy"))
    mine = jnp.dot(stiffness_inverse_lines, total, precision=highest)
    return lax.all_gather(mine, ("sx", "sy"), axis=0, tiled=True)


def inner(first, second):
    return jnp.sum(first * second, axis=0)


def shards(loads, schur_flex, dirichlet, coupling, corner_index, face_lists, coarse_inverse):
    highest = lax.Precision.HIGHEST
    flex_mat = schur_flex[0, 0]
    prec_mat = dirichlet[0, 0]
    coupling_mat = coupling[0, 0]
    corners = corner_index[0, 0]
    face_index = face_lists[0, 0]
    ncoarse = coarse_inverse.shape[1]
    onehot = (corners[None, :] == jnp.arange(ncoarse, dtype=jnp.int32)[:, None]).astype(jnp.float32)

    def precondition(dual_vector):
        spread = jump(dual_vector, face_index)
        operator_applied = jnp.dot(prec_mat, spread, precision=highest)
        return 0.5 * jump(operator_applied, face_index)

    def residual_dot(residual, precond):
        return lax.psum(inner(residual, precond), ("sx", "sy"))

    force_discontinuity = jump(loads[0, 0], face_index)
    multipliers = jnp.zeros_like(force_discontinuity)
    residual = force_discontinuity
    precond = precondition(residual)
    direction = precond
    residual_inner = residual_dot(residual, precond)
    for iteration in range(ITERS):
        width = direction.shape[1]
        apply_spread = jump(direction, face_index)
        fine_part = jnp.dot(flex_mat, apply_spread, precision=highest)
        local_load = jnp.dot(coupling_mat, apply_spread, precision=highest)
        coarse_rhs = jnp.dot(onehot, local_load, precision=highest)
        coarse_sol = coarse_solve(coarse_rhs, coarse_inverse)
        filled_out = jnp.concatenate([coarse_sol, jnp.zeros((1, width), jnp.float32)], axis=0)
        picked = filled_out[corners]
        correction = lax.dot_general(
            coupling_mat, picked, (((0,), (0,)), ((), ())), precision=highest
        )
        image_dir = jump(fine_part + correction, face_index)
        step_size = residual_inner / lax.psum(inner(direction, image_dir), ("sx", "sy"))
        multipliers = multipliers + step_size * direction
        residual = residual - step_size * image_dir
        if iteration + 1 < ITERS:
            precond = precondition(residual)
            new_dot = residual_dot(residual, precond)
            direction = precond + new_dot / residual_inner * direction
            residual_inner = new_dot
    return (multipliers[None, None], residual[None, None])


def solution(mesh):
    return jax.shard_map(
        shards,
        mesh=mesh,
        in_specs=(
            P("sx", "sy", None, None),
            P("sx", "sy", None, None),
            P("sx", "sy", None, None),
            P("sx", "sy", None, None),
            P("sx", "sy", None),
            P("sx", "sy", None, None),
            P(("sx", "sy"), None),
        ),
        out_specs=(P("sx", "sy", None, None), P("sx", "sy", None, None)),
        check_vma=False,
    )
```

profile of v0, /device:TPU:1, one launch (start us, length us, event | category | flops | bytes accessed | tf_op | source)
XLA Modules:
  0.0 1103.3 jit_solution(2738854772131072380)
XLA Ops:
  8.7 4.6 collective-permute-start
  15.2 3.6 collective-permute-start.2
  22.7 3.5 collective-permute-done.2
  26.2 4.1 collective-permute-done.3
  30.4 18.0 %gather_fusion = f32[1536,256]{1,0:T(8,128)} fusion(f32[4,384,256]{2,1,0:T(8,128)S(1)} %pad_maximum_fusion, s32[1536]{0:T(1024)S(1)} %reshape.175), kind=kCustom, calls=%fused_computation | custom fusion | bytes 3158016 | tf_op jit(solution)/shard_map/gather | solution.py:24
  51.4 5.1 collective-permute-start.4
  58.5 3.4 collective-permute-start.6
  63.2 2.8 collective-permute-done.5
  68.1 4.1 collective-permute-done.7
  72.3 18.0 %gather_fusion.1 = f32[1536,256]{1,0:T(8,128)} fusion(f32[4,384,256]{2,1,0:T(8,128)S(1)} %pad_maximum_fusion.1, s32[1536]{0:T(1024)S(1)} %reshape.175), kind=kCustom, calls=%fused_computation.1 | custom fusion | bytes 3158016 | tf_op jit(solution)/shard_map/gather | solution.py:24
  92.1 18.2 %fusion.10 = f32[1536,256]{0,1:T(8,128)S(1)} fusion(f32[1536,256]{1,0:T(8,128)S(1)} %bitcast.126, f32[1,1,1536,1536]{3,2,1,0:T(8,128)} %param.9), kind=kOutput, calls=%fused_computation.23 | convolution fusion | flops 7247757312 | bytes 12582912 | tf_op jit(solution)/shard_map/dot_general | solution.py:51
  110.3 5.9 collective-permute-start.8
  118.2 3.9 collective-permute-start.10
  126.9 4.1 collective-permute-done.11
  134.2 18.0 %gather_fusion.2 = f32[1536,256]{1,0:T(8,128)} fusion(f32[4,384,256]{2,1,0:T(8,128)S(1)} %copy.27, s32[1536]{0:T(1024)S(1)} %reshape.175), kind=kCustom, calls=%fused_computation.2 | custom fusion | bytes 3158016 | tf_op jit(solution)/shard_map/gather | solution.py:24
  152.2 3.1 copy.28
  157.2 6.4 collective-permute-start.12
  165.6 4.0 collective-permute-start.14
  174.3 3.9 collective-permute-done.15
  181.3 18.0 %gather_fusion.3 = f32[1536,256]{1,0:T(8,128)} fusion(f32[4,384,256]{2,1,0:T(8,128)S(1)} %copy.31, s32[1536]{0:T(1024)S(1)} %reshape.175), kind=kCustom, calls=%fused_computation.3 | custom fusion | bytes 3158016 | tf_op jit(solution)/shard_map/gather | solution.py:24
  203.9 11.6 %fusion.2 = f32[256,1536]{1,0:T(8,128)} fusion(f32[1,1,1536,1536]{3,2,1,0:T(8,128)} %param.8, f32[1536,256]{0,1:T(8,128)S(1)} %copy.32, f32[1536,256]{0,1:T(8,128)S(1)} %get-tuple-element.16), kind=kOutput, calls=%fused_computation.13 | convolution fusion | flops 7248543744 | bytes 14155776 | tf_op jit(solution)/shard_map/dot_general | solution.py:66
  215.4 139.1 %all-reduce.6.cloned.1.call-done = f32[512,256]{1,0:T(8,128)} async-done(((f32[512,256]{1,0:T(8,128)}), f32[512,256]{1,0:T(8,128)}) %all-reduce.6.cloned.1.call-update) | async-done | bytes 524304 | tf_op jit(solution)/shard_map/psum | solution.py:30
  355.9 54.6 %all-gather = f32[128,4,256]{2,1,0:T(4,128)} all-gather(f32[1,4,256]{2,1,0:T(4,128)S(1)} %convolution_bitcast_fusion.1), channel_id=1, replica_groups=mesh['sx'=8,'sy'=16] {'sx','sy'}, dimensions={0}, use_global_device_ids=true | all-gather | bytes 528384 | tf_op jit(solution)/shard_map/all_gather | solution.py:32
  421.0 3.1 collective-permute-start.17
  424.2 2.7 collective-permute-start.18
  429.8 3.0 copy.30
  435.2 4.9 collective-permute-done.19
  440.1 2.6 pad_maximum_fusion.4
  444.6 18.0 %gather_fusion.5 = f32[1536,256]{1,0:T(8,128)} fusion(f32[4,384,256]{2,1,0:T(8,128)S(1)} %copy.33, s32[1536]{0:T(1024)S(1)} %reshape.175), kind=kCustom, calls=%fused_computation.5 | custom fusion | bytes 3158016 | tf_op jit(solution)/shard_map/gather | solution.py:24
  462.6 3.2 copy.34
  465.8 3.8 multiply_reduce_fusion.2
  469.6 66.2 %all-reduce.2 = (f32[256]{0:T(256)S(1)}, f32[256]{0:T(256)S(1)}) all-reduce(f32[256]{0:T(256)S(1)} %get-tuple-element.7, f32[256]{0:T(256)S(1)} %get-tuple-element.6), channel_id=1, replica_groups=mesh['sx'=8,'sy'=16] {'sx','sy'}, use_global_device_ids=true, to_apply=%region_1.0 | all-reduce | flops 512 | bytes 4096 | tf_op jit(solution)/shard_map/psum | solution.py:55
  535.9 2.6 multiply_subtract_fusion
  539.6 3.3 collective-permute-start.20
  548.0 4.3 collective-permute-done.21
  552.3 3.0 collective-permute-done.22
  555.3 4.1 collective-permute-done.23
  562.5 18.0 %gather_fusion.6 = f32[1536,256]{1,0:T(8,128)} fusion(f32[4,384,256]{2,1,0:T(8,128)S(1)} %copy.35, s32[1536]{0:T(1024)S(1)} %reshape.175), kind=kCustom, calls=%fused_computation.6 | custom fusion | bytes 3158016 | tf_op jit(solution)/shard_map/gather | solution.py:24
  580.6 3.2 copy.36
  583.7 11.3 %fusion.13 = f32[1536,256]{0,1:T(8,128)S(1)} fusion(f32[1,1,1536,1536]{3,2,1,0:T(8,128)} %param.9, f32[1536,256]{0,1:T(8,128)S(1)} %copy-done.5, f32[1536,256]{0,1:T(8,128)} %copy.36), kind=kOutput, calls=%fused_computation.24 | convolution fusion | flops 7248150528 | bytes 14155776 | tf_op jit(solution)/shard_map/dot_general | solution.py:51
  596.2 3.4 collective-permute-start.24
  605.1 3.9 collective-permute-done.25
  611.5 4.1 collective-permute-done.27
  618.8 18.0 %gather_fusion.7 = f32[1536,256]{1,0:T(8,128)} fusion(f32[4,384,256]{2,1,0:T(8,128)S(1)} %copy.37, s32[1536]{0:T(1024)S(1)} %reshape.175), kind=kCustom, calls=%fused_computation.7 | custom fusion | bytes 3158016 | tf_op jit(solution)/shard_map/gather | solution.py:24
  636.7 3.1 copy.38
  642.2 69.1 %psum.45 = f32[256]{0:T(256)S(1)} all-reduce(f32[256]{0:T(256)S(1)} %multiply_reduce_fusion.1), channel_id=1, replica_groups=mesh['sx'=8,'sy'=16] {'sx','sy'}, use_global_device_ids=true, to_apply=%region_6.0 | all-reduce | flops 256 | bytes 2048 | tf_op jit(solution)/shard_map/psum | solution.py:55
  714.7 3.9 collective-permute-start.28
  723.7 4.3 collective-permute-done.29
  729.7 4.1 collective-permute-done.31
  737.0 18.0 %gather_fusion.8 = f32[1536,256]{1,0:T(8,128)} fusion(f32[4,384,256]{2,1,0:T(8,128)S(1)} %copy.39, s32[1536]{0:T(1024)S(1)} %reshape.175), kind=kCustom, calls=%fused_computation.8 | custom fusion | bytes 3158016 | tf_op jit(solution)/shard_map/gather | solution.py:24
  754.9 3.1 copy.40
  758.1 2.8 fusion.17
  762.1 12.2 %fusion = f32[256,1536]{1,0:T(8,128)} fusion(f32[1,1,1536,1536]{3,2,1,0:T(8,128)} %param.8, f32[1536,256]{0,1:T(8,128)S(1)} %copy-done.2, f32[1536,256]{0,1:T(8,128)} %copy.40), kind=kOutput, calls=%fused_computation.11 | convolution fusion | flops 7248150528 | bytes 14155776 | tf_op jit(solution)/shard_map/dot_general | solution.py:66
  774.3 135.6 %all-reduce.8.cloned.1.call-done = f32[512,256]{1,0:T(8,128)} async-done(((f32[512,256]{1,0:T(8,128)}), f32[512,256]{1,0:T(8,128)}) %all-reduce.8.cloned.1.call-update) | async-done | bytes 524304 | tf_op jit(solution)/shard_map/psum | solution.py:30
  911.3 54.2 %all-gather.1 = f32[128,4,256]{2,1,0:T(4,128)} all-gather(f32[1,4,256]{2,1,0:T(4,128)S(1)} %convolution_bitcast_fusion), channel_id=1, replica_groups=mesh['sx'=8,'sy'=16] {'sx','sy'}, dimensions={0}, use_global_device_ids=true | all-gather | bytes 528384 | tf_op jit(solution)/shard_map/all_gather | solution.py:32
  981.4 3.5 collective-permute-done.33
  984.9 3.8 collective-permute-done.34
  988.7 4.1 collective-permute-done.35
  995.9 18.0 %gather_fusion.10 = f32[1536,256]{1,0:T(8,128)} fusion(f32[4,384,256]{2,1,0:T(8,128)S(1)} %copy.41, s32[1536]{0:T(1024)S(1)} %reshape.175), kind=kCustom, calls=%fused_computation.10 | custom fusion | bytes 3158016 | tf_op jit(solution)/shard_map/gather | solution.py:24
  1013.9 3.1 copy.42
  1017.0 3.4 multiply_reduce_fusion
  1020.4 66.7 %psum.47 = f32[256]{0:T(256)S(1)} all-reduce(f32[256]{0:T(256)S(1)} %get-tuple-element.12), channel_id=1, replica_groups=mesh['sx'=8,'sy'=16] {'sx','sy'}, use_global_device_ids=true, to_apply=%region_9.0 | all-reduce | flops 256 | bytes 2048 | tf_op jit(solution)/shard_map/psum | solution.py:76
  1087.1 4.1 subtract_bitcast_fusion
  1091.2 3.1 copy.43
  (140 shorter events, 123.0 us)
Async XLA Ops:
  7.2 194.1 %copy-start = (f32[1,1,16,1536]{3,2,1,0:T(8,128)S(1)}, f32[1,1,16,1536]{3,2,1,0:T(8,128)}, u32[]{:S(2)}) copy-start(f32[1,1,16,1536]{3,2,1,0:T(8,128)} %param.10) | copy-start | bytes 294916
  7.2 12.9 %copy-start.19 = (s32[1,1,4,384]{3,2,1,0:T(4,128)S(1)}, s32[1,1,4,384]{3,2,1,0:T(4,128)}, u32[]{:S(2)}) copy-start(s32[1,1,4,384]{3,2,1,0:T(4,128)} %param.12) | copy-start | bytes 18436
  7.2 347.3 %all-reduce.6.cloned.1.call-start = ((), (), s32[]{:S(2)}) async-start(), calls=%async_computation | async-start | bytes 1048576 | tf_op jit(solution)/shard_map/psum | solution.py:30
  8.7 11.4 %collective-permute-start = (f32[384,256]{1,0:T(8,128)S(1)}, f32[384,256]{1,0:T(8,128)S(1)}, u32[]{:S(2)}, u32[]{:S(2)}) collective-permute-start(f32[384,256]{1,0:T(8,128)S(1)} %get-tuple-element.49), channel_id=1, source_target_pairs={{0,16},{16,32},{32,48},{48,64},{64,80},{80,96},{96,112},{1,17},{17... | collective-permute-start | bytes 1179656 | tf_op jit(solution)/shard_map/ppermute | solution.py:12
  13.3 9.4 collective-permute-start.1
  15.2 11.0 collective-permute-start.2
  18.8 11.5 %collective-permute-start.3 = (f32[384,256]{1,0:T(8,128)S(1)}, f32[384,256]{1,0:T(8,128)S(1)}, u32[]{:S(2)}, u32[]{:S(2)}) collective-permute-start(f32[384,256]{1,0:T(8,128)S(1)} %get-tuple-element.52), channel_id=1, source_target_pairs={{1,0},{2,1},{3,2},{4,3},{5,4},{6,5},{7,6},{8,7},{9,8},{10,9},{11,1... | collective-permute-start | bytes 1179656 | tf_op jit(solution)/shard_map/ppermute | solution.py:12
  30.4 18.0 %copy-start.10 = (f32[1,1,1536,256]{3,2,1,0:T(8,128)S(1)}, f32[1,1,1536,256]{3,2,1,0:T(8,128)}, u32[]{:S(2)}) copy-start(f32[1,1,1536,256]{3,2,1,0:T(8,128)} %param.7) | copy-start | bytes 4718596
  50.3 1.1 copy-start.12
  51.4 11.8 %collective-permute-start.4 = (f32[384,256]{1,0:T(8,128)S(1)}, f32[384,256]{1,0:T(8,128)S(1)}, u32[]{:S(2)}, u32[]{:S(2)}) collective-permute-start(f32[384,256]{1,0:T(8,128)S(1)} %get-tuple-element.45), channel_id=1, source_target_pairs={{0,16},{16,32},{32,48},{48,64},{64,80},{80,96},{96,112},{1,17},{17... | collective-permute-start | bytes 1179656 | tf_op jit(solution)/shard_map/ppermute | solution.py:12
  56.6 9.4 collective-permute-start.5
  58.5 9.6 collective-permute-start.6
  61.9 10.3 collective-permute-start.7
  72.3 18.0 %copy-start.13 = (f32[4,384,256]{2,1,0:T(8,128)S(1)}, f32[4,384,256]{2,1,0:T(8,128)}, u32[]{:S(2)}) copy-start(f32[4,384,256]{2,1,0:T(8,128)} %copy-done.12) | copy-start | bytes 4718596
  110.3 13.3 %collective-permute-start.8 = (f32[384,256]{0,1:T(8,128)S(1)}, f32[384,256]{0,1:T(8,128)S(1)}, u32[]{:S(2)}, u32[]{:S(2)}) collective-permute-start(f32[384,256]{0,1:T(8,128)S(1)} %get-tuple-element.41), channel_id=1, source_target_pairs={{0,16},{16,32},{32,48},{48,64},{64,80},{80,96},{96,112},{1,17},{17... | collective-permute-start | bytes 1179656 | tf_op jit(solution)/shard_map/ppermute | solution.py:12
  116.3 9.4 collective-permute-start.9
  118.2 8.7 collective-permute-start.10
  122.1 8.9 collective-permute-start.11
  157.1 13.8 %copy-start.20 = (s32[1,1,16]{2,1,0:T(1,128)S(1)}, s32[1,1,16]{2,1,0:T(1,128)}, u32[]{:S(2)}) copy-start(s32[1,1,16]{2,1,0:T(1,128)} %param.11) | copy-start | bytes 196
  157.2 13.8 %collective-permute-start.12 = (f32[384,256]{0,1:T(8,128)S(1)}, f32[384,256]{0,1:T(8,128)S(1)}, u32[]{:S(2)}, u32[]{:S(2)}) collective-permute-start(f32[384,256]{0,1:T(8,128)S(1)} %get-tuple-element.37), channel_id=1, source_target_pairs={{0,16},{16,32},{32,48},{48,64},{64,80},{80,96},{96,112},{1,17},{17... | collective-permute-start | bytes 1179656 | tf_op jit(solution)/shard_map/ppermute | solution.py:12
  163.7 9.4 collective-permute-start.13
  165.6 8.7 collective-permute-start.14
  169.6 8.6 collective-permute-start.15
  203.8 150.7 %copy-start.18 = (f32[4,512]{1,0:T(4,128)S(1)}, f32[4,512]{1,0:T(4,128)}, u32[]{:S(2)}) copy-start(f32[4,512]{1,0:T(4,128)} %param.13) | copy-start | bytes 24580
  203.8 706.1 %all-reduce.8.cloned.1.call-start = ((), (), s32[]{:S(2)}) async-start(), calls=%async_computation.1 | async-start | bytes 1048576 | tf_op jit(solution)/shard_map/psum | solution.py:30
  215.4 200.5 %copy-start.16 = (f32[256,1536]{1,0:T(8,128)S(1)}, f32[256,1536]{1,0:T(8,128)}, u32[]{:S(2)}) copy-start(f32[256,1536]{1,0:T(8,128)} %fusion.2) | copy-start | bytes 4718596
  417.4 1.7 copy-start.8
  417.4 10.8 copy-start.11
  419.1 13.7 %collective-permute-start.16 = (f32[384,256]{0,1:T(8,128)}, f32[384,256]{0,1:T(8,128)}, u32[]{:S(2)}, u32[]{:S(2)}) collective-permute-start(f32[384,256]{0,1:T(8,128)} %get-tuple-element.33), channel_id=1, source_target_pairs={{0,16},{16,32},{32,48},{48,64},{64,80},{80,96},{96,112},{1,17},{17... | collective-permute-start | bytes 1179656 | tf_op jit(solution)/shard_map/ppermute | solution.py:12
  421.0 11.8 %collective-permute-start.17 = (f32[384,256]{0,1:T(8,128)}, f32[384,256]{0,1:T(8,128)}, u32[]{:S(2)}, u32[]{:S(2)}) collective-permute-start(f32[384,256]{0,1:T(8,128)} %get-tuple-element.36), channel_id=1, source_target_pairs={{16,0},{32,16},{48,32},{64,48},{80,64},{96,80},{112,96},{17,1},{33... | collective-permute-start | bytes 1179656 | tf_op jit(solution)/shard_map/ppermute | solution.py:12
  424.2 11.1 %collective-permute-start.18 = (f32[384,256]{0,1:T(8,128)}, f32[384,256]{0,1:T(8,128)}, u32[]{:S(2)}, u32[]{:S(2)}) collective-permute-start(f32[384,256]{0,1:T(8,128)} %get-tuple-element.35), channel_id=1, source_target_pairs={{0,1},{1,2},{2,3},{3,4},{4,5},{5,6},{6,7},{7,8},{8,9},{9,10},{10,1... | collective-permute-start | bytes 1179656 | tf_op jit(solution)/shard_map/ppermute | solution.py:12
  426.9 13.2 %collective-permute-start.19 = (f32[384,256]{0,1:T(8,128)}, f32[384,256]{0,1:T(8,128)}, u32[]{:S(2)}, u32[]{:S(2)}) collective-permute-start(f32[384,256]{0,1:T(8,128)} %get-tuple-element.34), channel_id=1, source_target_pairs={{1,0},{2,1},{3,2},{4,3},{5,4},{6,5},{7,6},{8,7},{9,8},{10,9},{11,1... | collective-permute-start | bytes 1179656 | tf_op jit(solution)/shard_map/ppermute | solution.py:12
  462.6 3.2 copy-start.9
  538.5 1.1 copy-start.4
  539.6 8.3 collective-permute-start.20
  542.9 9.4 collective-permute-start.21
  544.8 10.5 collective-permute-start.22
  546.5 12.9 %collective-permute-start.23 = (f32[384,256]{0,1:T(8,128)S(1)}, f32[384,256]{0,1:T(8,128)S(1)}, u32[]{:S(2)}, u32[]{:S(2)}) collective-permute-start(f32[384,256]{0,1:T(8,128)S(1)} %get-tuple-element.30), channel_id=1, source_target_pairs={{1,0},{2,1},{3,2},{4,3},{5,4},{6,5},{7,6},{8,7},{9,8},{10,9},{11,1... | collective-permute-start | bytes 1179656 | tf_op jit(solution)/shard_map/ppermute | solution.py:12
  580.5 3.2 copy-start.5
  595.0 1.1 copy-start.7
  596.2 9.0 collective-permute-start.24
  599.6 9.4 collective-permute-start.25
  601.5 9.9 collective-permute-start.26
  603.8 11.8 %collective-permute-start.27 = (f32[384,256]{0,1:T(8,128)S(1)}, f32[384,256]{0,1:T(8,128)S(1)}, u32[]{:S(2)}, u32[]{:S(2)}) collective-permute-start(f32[384,256]{0,1:T(8,128)S(1)} %get-tuple-element.26), channel_id=1, source_target_pairs={{1,0},{2,1},{3,2},{4,3},{5,4},{6,5},{7,6},{8,7},{9,8},{10,9},{11,1... | collective-permute-start | bytes 1179656 | tf_op jit(solution)/shard_map/ppermute | solution.py:12
  636.7 3.1 copy-start.6
  713.5 1.1 copy-start.1
  714.7 9.0 collective-permute-start.28
  718.5 9.4 collective-permute-start.29
  720.5 9.2 collective-permute-start.30
  722.1 11.7 %collective-permute-start.31 = (f32[384,256]{0,1:T(8,128)S(1)}, f32[384,256]{0,1:T(8,128)S(1)}, u32[]{:S(2)}, u32[]{:S(2)}) collective-permute-start(f32[384,256]{0,1:T(8,128)S(1)} %get-tuple-element.22), channel_id=1, source_target_pairs={{1,0},{2,1},{3,2},{4,3},{5,4},{6,5},{7,6},{8,7},{9,8},{10,9},{11,1... | collective-permute-start | bytes 1179656 | tf_op jit(solution)/shard_map/ppermute | solution.py:12
  754.9 3.1 copy-start.2
  774.3 196.7 %copy-start.15 = (f32[256,1536]{1,0:T(8,128)S(1)}, f32[256,1536]{1,0:T(8,128)}, u32[]{:S(2)}) copy-start(f32[256,1536]{1,0:T(8,128)} %fusion) | copy-start | bytes 4718596
  972.4 1.2 copy-start.14
  973.6 7.8 collective-permute-start.32
  975.5 9.4 collective-permute-start.33
  977.9 10.7 collective-permute-start.34
  979.9 12.9 %collective-permute-start.35 = (f32[384,256]{0,1:T(8,128)S(1)}, f32[384,256]{0,1:T(8,128)S(1)}, u32[]{:S(2)}, u32[]{:S(2)}) collective-permute-start(f32[384,256]{0,1:T(8,128)S(1)} %get-tuple-element.18), channel_id=1, source_target_pairs={{1,0},{2,1},{3,2},{4,3},{5,4},{6,5},{7,6},{8,7},{9,8},{10,9},{11,1... | collective-permute-start | bytes 1179656 | tf_op jit(solution)/shard_map/ppermute | solution.py:12
  1013.9 3.1 copy-start.3
  1091.2 3.1 copy-start.17
Sparse Core Ops, SparseCore 0:
  203.9 150.5 all-reduce.5
  762.2 147.6 all-reduce.7
where the time goes:
time: 1110 us; the launch traced here: 1100 us
  waiting for transfers between devices  359 us (32%)
  blocking collectives  311 us (28%)
  local copies, waits for them, and re-layouts  225 us (20%)
  starting transfers between devices  93.2 us (8%)
  matrix products  65.3 us (6%)
  other arithmetic  34.2 us (3%)
  between operations  15.2 us (1%)
    psum x2, waiting for transfers between devices, coarse_solve(): total = lax.psum(coarse_rhs, ('sx', 'sy'))  275 us
    gather x17, local copies, waits for them, and re-layouts, jump(): matched = received[jnp.arange(4, dtype=jnp.int32)[:, None], face_index]  186 us
    psum x2, blocking collectives, residual_dot(): return lax.psum(inner(residual, precond), ('sx', 'sy'))  135 us
    all_gather x2, blocking collectives, coarse_solve(): return lax.all_gather(mine, ('sx', 'sy'), axis=0, tiled=True)  109 us
    ppermute x36, starting transfers between devices, shifted(): return lax.ppermute(block, axis, route)  93.1 us
    ppermute x36, waiting for transfers between devices, shifted(): return lax.ppermute(block, axis, route)  84.4 us
    psum x1, blocking collectives, shards(): lax.psum(inner(direction, image_dir), ('sx', 'sy'))  66.7 us
    dot_general x2, matrix products, precondition(): operator_applied = jnp.dot(prec_mat, spread, precision=highest)  29.5 us
  transfers between devices with their start and end apart: 38, of which 28 were waited for; matrix products, arithmetic and copies ran while one was open for 3% of the time, Pallas kernels for 0%

commit v1 on v0

--- a/solution.py
+++ b/solution.py
@@ -2,6 +2,7 @@
 import jax.numpy as jnp
 from jax import lax
 from jax.sharding import PartitionSpec as P
+from jax.lax import all_gather
 
 ITERS = 2
 
@@ -73,7 +74,8 @@
             coupling_mat, picked, (((0,), (0,)), ((), ())), precision=highest
         )
         image_dir = jump(fine_part + correction, face_index)
-        step_size = residual_inner / lax.psum(inner(direction, image_dir), ("sx", "sy"))
+        lay_notes = lambda shard_in: all_gather(shard_in, axis_name=("sx", "sy")).sum(axis=0)
+        step_size = residual_inner / lay_notes(inner(direction, image_dir))
         multipliers = multipliers + step_size * direction
         residual = residual - step_size * image_dir
         if iteration + 1 < ITERS:

time: 1110 us -> 1150 us (1.036)
  blocking collectives: 311 us -> 345 us
    all_gather x0 -> x2, blocking collectives: none -> 104 us  [shards(): all_gather(shard_in, axis_name=('sx', 'sy')).sum(axis=0)]
    psum x1 -> x0, blocking collectives: 66.7 us -> none  [shards(): lax.psum(inner(direction, image_dir), ('sx', 'sy'))]
where the time goes in v1:
time: 1150 us; the launch traced here: 1140 us
  waiting for transfers between devices  359 us (31%)
  blocking collectives  345 us (30%)
  local copies, waits for them, and re-layouts  225 us (20%)
  starting transfers between devices  93 us (8%)
  matrix products  65.4 us (6%)
  other arithmetic  34.6 us (3%)
  between operations  15.2 us (1%)
    psum x2, waiting for transfers between devices, coarse_solve(): total = lax.psum(coarse_rhs, ('sx', 'sy'))  274 us
    gather x17, local copies, waits for them, and re-layouts, jump(): matched = received[jnp.arange(4, dtype=jnp.int32)[:, None], face_index]  186 us
    psum x2, blocking collectives, residual_dot(): return lax.psum(inner(residual, precond), ('sx', 'sy'))  132 us
    all_gather x2, blocking collectives, coarse_solve(): return lax.all_gather(mine, ('sx', 'sy'), axis=0, tiled=True)  109 us
    all_gather x2, blocking collectives, shards(): all_gather(shard_in, axis_name=('sx', 'sy')).sum(axis=0)  104 us
    ppermute x36, starting transfers between devices, shifted(): return lax.ppermute(block, axis, route)  92.9 us
    ppermute x36, waiting for transfers between devices, shifted(): return lax.ppermute(block, axis, route)  85.1 us
    dot_general x2, matrix products, precondition(): operator_applied = jnp.dot(prec_mat, spread, precision=highest)  29.5 us
  transfers between devices with their start and end apart: 38, of which 28 were waited for; matrix products, arithmetic and copies ran while one was open for 3% of the time, Pallas kernels for 0%

profile of v1, /device:TPU:1, one launch (start us, length us, event | category | flops | bytes accessed | tf_op | source)
XLA Modules:
  0.0 1137.9 jit_solution(9506597619995351646)
XLA Ops:
  8.7 4.6 collective-permute-start
  15.2 3.6 collective-permute-start.2
  22.7 3.5 collective-permute-done.2
  26.2 4.1 collective-permute-done.3
  30.4 18.0 %gather_fusion = f32[1536,256]{1,0:T(8,128)} fusion(f32[4,384,256]{2,1,0:T(8,128)S(1)} %pad_maximum_fusion, s32[1536]{0:T(1024)S(1)} %reshape.175), kind=kCustom, calls=%fused_computation | custom fusion | bytes 3158016 | tf_op jit(solution)/shard_map/gather | solution.py:25
  51.4 5.1 collective-permute-start.4
  58.5 3.4 collective-permute-start.6
  63.2 2.8 collective-permute-done.5
  68.1 4.1 collective-permute-done.7
  72.3 18.0 %gather_fusion.1 = f32[1536,256]{1,0:T(8,128)} fusion(f32[4,384,256]{2,1,0:T(8,128)S(1)} %pad_maximum_fusion.1, s32[1536]{0:T(1024)S(1)} %reshape.175), kind=kCustom, calls=%fused_computation.1 | custom fusion | bytes 3158016 | tf_op jit(solution)/shard_map/gather | solution.py:25
  92.1 18.2 %fusion.10 = f32[1536,256]{0,1:T(8,128)S(1)} fusion(f32[1536,256]{1,0:T(8,128)S(1)} %bitcast.128, f32[1,1,1536,1536]{3,2,1,0:T(8,128)} %param.9), kind=kOutput, calls=%fused_computation.23 | convolution fusion | flops 7247757312 | bytes 12582912 | tf_op jit(solution)/shard_map/dot_general | solution.py:52
  110.4 5.9 collective-permute-start.8
  118.2 3.9 collective-permute-start.10
  126.9 4.1 collective-permute-done.11
  134.2 18.0 %gather_fusion.2 = f32[1536,256]{1,0:T(8,128)} fusion(f32[4,384,256]{2,1,0:T(8,128)S(1)} %copy.27, s32[1536]{0:T(1024)S(1)} %reshape.175), kind=kCustom, calls=%fused_computation.2 | custom fusion | bytes 3158016 | tf_op jit(solution)/shard_map/gather | solution.py:25
  152.2 3.1 copy.28
  157.2 6.4 collective-permute-start.12
  165.6 4.0 collective-permute-start.14
  174.3 3.9 collective-permute-done.15
  181.3 18.0 %gather_fusion.3 = f32[1536,256]{1,0:T(8,128)} fusion(f32[4,384,256]{2,1,0:T(8,128)S(1)} %copy.31, s32[1536]{0:T(1024)S(1)} %reshape.175), kind=kCustom, calls=%fused_computation.3 | custom fusion | bytes 3158016 | tf_op jit(solution)/shard_map/gather | solution.py:25
  203.9 11.6 %fusion.2 = f32[256,1536]{1,0:T(8,128)} fusion(f32[1,1,1536,1536]{3,2,1,0:T(8,128)} %param.8, f32[1536,256]{0,1:T(8,128)S(1)} %copy.32, f32[1536,256]{0,1:T(8,128)S(1)} %get-tuple-element.14), kind=kOutput, calls=%fused_computation.13 | convolution fusion | flops 7248543744 | bytes 14155776 | tf_op jit(solution)/shard_map/dot_general | solution.py:67
  215.5 139.1 %all-reduce.5.cloned.1.call-done = f32[512,256]{1,0:T(8,128)} async-done(((f32[512,256]{1,0:T(8,128)}), f32[512,256]{1,0:T(8,128)}) %all-reduce.5.cloned.1.call-update) | async-done | bytes 524304 | tf_op jit(solution)/shard_map/psum | solution.py:31
  355.9 54.6 %all-gather.2 = f32[128,4,256]{2,1,0:T(4,128)} all-gather(f32[1,4,256]{2,1,0:T(4,128)S(1)} %convolution_bitcast_fusion.1), channel_id=1, replica_groups=mesh['sx'=8,'sy'=16] {'sx','sy'}, dimensions={0}, use_global_device_ids=true | all-gather | bytes 528384 | tf_op jit(solution)/shard_map/all_gather | solution.py:33
  421.1 3.1 collective-permute-start.17
  424.3 2.7 collective-permute-start.18
  429.9 3.0 copy.30
  435.3 4.9 collective-permute-done.19
  444.7 18.0 %gather_fusion.5 = f32[1536,256]{1,0:T(8,128)} fusion(f32[4,384,256]{2,1,0:T(8,128)S(1)} %copy.33, s32[1536]{0:T(1024)S(1)} %reshape.175), kind=kCustom, calls=%fused_computation.5 | custom fusion | bytes 3158016 | tf_op jit(solution)/shard_map/gather | solution.py:25
  462.7 3.2 copy.34
  465.8 3.8 multiply_reduce_fusion.2
  469.7 52.0 %all-gather.3 = f32[128,1,256]{2,1,0:T(1,128)S(1)} all-gather(f32[1,1,256]{2,1,0:T(1,128)S(1)} %bitcast.161), channel_id=2, replica_groups=mesh['sx'=8,'sy'=16] {'sx','sy'}, dimensions={0}, use_global_device_ids=true | all-gather | bytes 132096 | tf_op jit(solution)/shard_map/all_gather | solution.py:77
  521.9 64.4 %psum.28 = f32[256]{0:T(256)S(1)} all-reduce(f32[256]{0:T(256)S(1)} %get-tuple-element.7), channel_id=1, replica_groups=mesh['sx'=8,'sy'=16] {'sx','sy'}, use_global_device_ids=true, to_apply=%region_1.0 | all-reduce | flops 256 | bytes 2048 | tf_op jit(solution)/shard_map/psum | solution.py:56
  586.3 2.6 multiply_subtract_fusion
  598.1 3.9 collective-permute-done.21
  602.0 3.2 collective-permute-done.22
  605.2 4.4 collective-permute-done.23
  612.7 18.0 %gather_fusion.6 = f32[1536,256]{1,0:T(8,128)} fusion(f32[4,384,256]{2,1,0:T(8,128)S(1)} %copy.35, s32[1536]{0:T(1024)S(1)} %reshape.175), kind=kCustom, calls=%fused_computation.6 | custom fusion | bytes 3158016 | tf_op jit(solution)/shard_map/gather | solution.py:25
  630.7 3.2 copy.36
  633.9 11.3 fusion.13
  646.3 3.2 collective-permute-start.24
  655.2 3.8 collective-permute-done.25
  658.9 3.0 collective-permute-done.26
  661.9 4.1 collective-permute-done.27
  669.2 18.0 %gather_fusion.7 = f32[1536,256]{1,0:T(8,128)} fusion(f32[4,384,256]{2,1,0:T(8,128)S(1)} %copy.37, s32[1536]{0:T(1024)S(1)} %reshape.175), kind=kCustom, calls=%fused_computation.7 | custom fusion | bytes 3158016 | tf_op jit(solution)/shard_map/gather | solution.py:25
  687.2 3.2 copy.38
  692.7 67.7 %psum.30 = f32[256]{0:T(256)S(1)} all-reduce(f32[256]{0:T(256)S(1)} %multiply_reduce_fusion.1), channel_id=1, replica_groups=mesh['sx'=8,'sy'=16] {'sx','sy'}, use_global_device_ids=true, to_apply=%region_6.0 | all-reduce | flops 256 | bytes 2048 | tf_op jit(solution)/shard_map/psum | solution.py:56
  763.7 4.4 collective-permute-start.28
  772.9 4.6 collective-permute-done.29
  779.3 4.1 collective-permute-done.31
  786.5 18.0 %gather_fusion.8 = f32[1536,256]{1,0:T(8,128)} fusion(f32[4,384,256]{2,1,0:T(8,128)S(1)} %copy.39, s32[1536]{0:T(1024)S(1)} %reshape.175), kind=kCustom, calls=%fused_computation.8 | custom fusion | bytes 3158016 | tf_op jit(solution)/shard_map/gather | solution.py:25
  804.5 3.2 copy.40
  807.7 2.8 fusion.17
  811.7 12.2 %fusion = f32[256,1536]{1,0:T(8,128)} fusion(f32[1,1,1536,1536]{3,2,1,0:T(8,128)} %param.8, f32[1536,256]{0,1:T(8,128)S(1)} %copy-done.2, f32[1536,256]{0,1:T(8,128)} %copy.40), kind=kOutput, calls=%fused_computation.11 | convolution fusion | flops 7248150528 | bytes 14155776 | tf_op jit(solution)/shard_map/dot_general | solution.py:67
  823.9 135.1 %all-reduce.7.cloned.1.call-done = f32[512,256]{1,0:T(8,128)} async-done(((f32[512,256]{1,0:T(8,128)}), f32[512,256]{1,0:T(8,128)}) %all-reduce.7.cloned.1.call-update) | async-done | bytes 524304 | tf_op jit(solution)/shard_map/psum | solution.py:31
  960.4 54.2 %all-gather.4 = f32[128,4,256]{2,1,0:T(4,128)} all-gather(f32[1,4,256]{2,1,0:T(4,128)S(1)} %convolution_bitcast_fusion), channel_id=1, replica_groups=mesh['sx'=8,'sy'=16] {'sx','sy'}, dimensions={0}, use_global_device_ids=true | all-gather | bytes 528384 | tf_op jit(solution)/shard_map/all_gather | solution.py:33
  1030.7 3.4 collective-permute-done.33
  1034.1 3.9 collective-permute-done.34
  1037.9 4.1 collective-permute-done.35
  1045.2 17.9 %gather_fusion.10 = f32[1536,256]{1,0:T(8,128)} fusion(f32[4,384,256]{2,1,0:T(8,128)S(1)} %copy.41, s32[1536]{0:T(1024)S(1)} %reshape.175), kind=kCustom, calls=%fused_computation.10 | custom fusion | bytes 3158016 | tf_op jit(solution)/shard_map/gather | solution.py:25
  1063.1 3.2 copy.42
  1066.3 3.4 multiply_reduce_fusion
  1069.6 52.0 %all-gather.5 = f32[128,1,256]{2,1,0:T(1,128)S(1)} all-gather(f32[1,1,256]{2,1,0:T(1,128)S(1)} %bitcast.162), channel_id=3, replica_groups=mesh['sx'=8,'sy'=16] {'sx','sy'}, dimensions={0}, use_global_device_ids=true | all-gather | bytes 132096 | tf_op jit(solution)/shard_map/all_gather | solution.py:77
  1121.8 4.1 subtract_bitcast_fusion
  1125.9 3.1 copy.43
  (143 shorter events, 126.3 us)
Async XLA Ops:
  7.2 194.1 %copy-start = (f32[1,1,16,1536]{3,2,1,0:T(8,128)S(1)}, f32[1,1,16,1536]{3,2,1,0:T(8,128)}, u32[]{:S(2)}) copy-start(f32[1,1,16,1536]{3,2,1,0:T(8,128)} %param.10) | copy-start | bytes 294916
  7.2 12.9 %copy-start.19 = (s32[1,1,4,384]{3,2,1,0:T(4,128)S(1)}, s32[1,1,4,384]{3,2,1,0:T(4,128)}, u32[]{:S(2)}) copy-start(s32[1,1,4,384]{3,2,1,0:T(4,128)} %param.12) | copy-start | bytes 18436
  7.2 347.4 %all-reduce.5.cloned.1.call-start = ((), (), s32[]{:S(2)}) async-start(), calls=%async_computation | async-start | bytes 1048576 | tf_op jit(solution)/shard_map/psum | solution.py:31
  8.7 11.4 %collective-permute-start = (f32[384,256]{1,0:T(8,128)S(1)}, f32[384,256]{1,0:T(8,128)S(1)}, u32[]{:S(2)}, u32[]{:S(2)}) collective-permute-start(f32[384,256]{1,0:T(8,128)S(1)} %get-tuple-element.47), channel_id=1, source_target_pairs={{0,16},{16,32},{32,48},{48,64},{64,80},{80,96},{96,112},{1,17},{17... | collective-permute-start | bytes 1179656 | tf_op jit(solution)/shard_map/ppermute | solution.py:13
  13.3 9.4 collective-permute-start.1
  15.2 11.0 collective-permute-start.2
  18.8 11.5 %collective-permute-start.3 = (f32[384,256]{1,0:T(8,128)S(1)}, f32[384,256]{1,0:T(8,128)S(1)}, u32[]{:S(2)}, u32[]{:S(2)}) collective-permute-start(f32[384,256]{1,0:T(8,128)S(1)} %get-tuple-element.50), channel_id=1, source_target_pairs={{1,0},{2,1},{3,2},{4,3},{5,4},{6,5},{7,6},{8,7},{9,8},{10,9},{11,1... | collective-permute-start | bytes 1179656 | tf_op jit(solution)/shard_map/ppermute | solution.py:13
  30.4 18.0 %copy-start.10 = (f32[1,1,1536,256]{3,2,1,0:T(8,128)S(1)}, f32[1,1,1536,256]{3,2,1,0:T(8,128)}, u32[]{:S(2)}) copy-start(f32[1,1,1536,256]{3,2,1,0:T(8,128)} %param.7) | copy-start | bytes 4718596
  50.3 1.1 copy-start.12
  51.4 11.8 %collective-permute-start.4 = (f32[384,256]{1,0:T(8,128)S(1)}, f32[384,256]{1,0:T(8,128)S(1)}, u32[]{:S(2)}, u32[]{:S(2)}) collective-permute-start(f32[384,256]{1,0:T(8,128)S(1)} %get-tuple-element.43), channel_id=1, source_target_pairs={{0,16},{16,32},{32,48},{48,64},{64,80},{80,96},{96,112},{1,17},{17... | collective-permute-start | bytes 1179656 | tf_op jit(solution)/shard_map/ppermute | solution.py:13
  56.6 9.4 collective-permute-start.5
  58.5 9.6 collective-permute-start.6
  61.9 10.3 collective-permute-start.7
  72.3 18.0 %copy-start.13 = (f32[4,384,256]{2,1,0:T(8,128)S(1)}, f32[4,384,256]{2,1,0:T(8,128)}, u32[]{:S(2)}) copy-start(f32[4,384,256]{2,1,0:T(8,128)} %copy-done.12) | copy-start | bytes 4718596
  110.4 13.3 %collective-permute-start.8 = (f32[384,256]{0,1:T(8,128)S(1)}, f32[384,256]{0,1:T(8,128)S(1)}, u32[]{:S(2)}, u32[]{:S(2)}) collective-permute-start(f32[384,256]{0,1:T(8,128)S(1)} %get-tuple-element.39), channel_id=1, source_target_pairs={{0,16},{16,32},{32,48},{48,64},{64,80},{80,96},{96,112},{1,17},{17... | collective-permute-start | bytes 1179656 | tf_op jit(solution)/shard_map/ppermute | solution.py:13
  116.3 9.4 collective-permute-start.9
  118.2 8.7 collective-permute-start.10
  122.2 8.9 collective-permute-start.11
  157.1 13.8 %copy-start.20 = (s32[1,1,16]{2,1,0:T(1,128)S(1)}, s32[1,1,16]{2,1,0:T(1,128)}, u32[]{:S(2)}) copy-start(s32[1,1,16]{2,1,0:T(1,128)} %param.11) | copy-start | bytes 196
  157.2 13.8 %collective-permute-start.12 = (f32[384,256]{0,1:T(8,128)S(1)}, f32[384,256]{0,1:T(8,128)S(1)}, u32[]{:S(2)}, u32[]{:S(2)}) collective-permute-start(f32[384,256]{0,1:T(8,128)S(1)} %get-tuple-element.35), channel_id=1, source_target_pairs={{0,16},{16,32},{32,48},{48,64},{64,80},{80,96},{96,112},{1,17},{17... | collective-permute-start | bytes 1179656 | tf_op jit(solution)/shard_map/ppermute | solution.py:13
  163.7 9.4 collective-permute-start.13
  165.6 8.7 collective-permute-start.14
  169.6 8.6 collective-permute-start.15
  203.8 150.7 %copy-start.18 = (f32[4,512]{1,0:T(4,128)S(1)}, f32[4,512]{1,0:T(4,128)}, u32[]{:S(2)}) copy-start(f32[4,512]{1,0:T(4,128)} %param.13) | copy-start | bytes 24580
  203.8 755.2 %all-reduce.7.cloned.1.call-start = ((), (), s32[]{:S(2)}) async-start(), calls=%async_computation.1 | async-start | bytes 1048576 | tf_op jit(solution)/shard_map/psum | solution.py:31
  215.5 200.6 %copy-start.16 = (f32[256,1536]{1,0:T(8,128)S(1)}, f32[256,1536]{1,0:T(8,128)}, u32[]{:S(2)}) copy-start(f32[256,1536]{1,0:T(8,128)} %fusion.2) | copy-start | bytes 4718596
  417.5 1.7 copy-start.8
  417.5 10.7 copy-start.11
  419.2 13.7 %collective-permute-start.16 = (f32[384,256]{0,1:T(8,128)}, f32[384,256]{0,1:T(8,128)}, u32[]{:S(2)}, u32[]{:S(2)}) collective-permute-start(f32[384,256]{0,1:T(8,128)} %get-tuple-element.31), channel_id=1, source_target_pairs={{0,16},{16,32},{32,48},{48,64},{64,80},{80,96},{96,112},{1,17},{17... | collective-permute-start | bytes 1179656 | tf_op jit(solution)/shard_map/ppermute | solution.py:13
  421.1 11.8 %collective-permute-start.17 = (f32[384,256]{0,1:T(8,128)}, f32[384,256]{0,1:T(8,128)}, u32[]{:S(2)}, u32[]{:S(2)}) collective-permute-start(f32[384,256]{0,1:T(8,128)} %get-tuple-element.34), channel_id=1, source_target_pairs={{16,0},{32,16},{48,32},{64,48},{80,64},{96,80},{112,96},{17,1},{33... | collective-permute-start | bytes 1179656 | tf_op jit(solution)/shard_map/ppermute | solution.py:13
  424.3 11.0 collective-permute-start.18
  427.0 13.2 %collective-permute-start.19 = (f32[384,256]{0,1:T(8,128)}, f32[384,256]{0,1:T(8,128)}, u32[]{:S(2)}, u32[]{:S(2)}) collective-permute-start(f32[384,256]{0,1:T(8,128)} %get-tuple-element.32), channel_id=1, source_target_pairs={{1,0},{2,1},{3,2},{4,3},{5,4},{6,5},{7,6},{8,7},{9,8},{10,9},{11,1... | collective-permute-start | bytes 1179656 | tf_op jit(solution)/shard_map/ppermute | solution.py:13
  462.7 3.2 copy-start.9
  589.0 1.1 copy-start.4
  590.1 8.0 collective-permute-start.20
  592.6 9.4 collective-permute-start.21
  594.5 10.7 collective-permute-start.22
  596.6 12.9 %collective-permute-start.23 = (f32[384,256]{0,1:T(8,128)S(1)}, f32[384,256]{0,1:T(8,128)S(1)}, u32[]{:S(2)}, u32[]{:S(2)}) collective-permute-start(f32[384,256]{0,1:T(8,128)S(1)} %get-tuple-element.28), channel_id=1, source_target_pairs={{1,0},{2,1},{3,2},{4,3},{5,4},{6,5},{7,6},{8,7},{9,8},{10,9},{11,1... | collective-permute-start | bytes 1179656 | tf_op jit(solution)/shard_map/ppermute | solution.py:13
  630.7 3.2 copy-start.5
  645.2 1.1 copy-start.7
  646.3 8.8 collective-permute-start.24
  649.5 9.4 collective-permute-start.25
  651.5 10.4 collective-permute-start.26
  653.9 12.2 %collective-permute-start.27 = (f32[384,256]{0,1:T(8,128)S(1)}, f32[384,256]{0,1:T(8,128)S(1)}, u32[]{:S(2)}, u32[]{:S(2)}) collective-permute-start(f32[384,256]{0,1:T(8,128)S(1)} %get-tuple-element.24), channel_id=1, source_target_pairs={{1,0},{2,1},{3,2},{4,3},{5,4},{6,5},{7,6},{8,7},{9,8},{10,9},{11,1... | collective-permute-start | bytes 1179656 | tf_op jit(solution)/shard_map/ppermute | solution.py:13
  687.2 3.2 copy-start.6
  762.6 1.1 copy-start.1
  763.7 9.2 collective-permute-start.28
  768.1 9.4 collective-permute-start.29
  770.1 9.2 collective-permute-start.30
  771.4 12.0 %collective-permute-start.31 = (f32[384,256]{0,1:T(8,128)S(1)}, f32[384,256]{0,1:T(8,128)S(1)}, u32[]{:S(2)}, u32[]{:S(2)}) collective-permute-start(f32[384,256]{0,1:T(8,128)S(1)} %get-tuple-element.20), channel_id=1, source_target_pairs={{1,0},{2,1},{3,2},{4,3},{5,4},{6,5},{7,6},{8,7},{9,8},{10,9},{11,1... | collective-permute-start | bytes 1179656 | tf_op jit(solution)/shard_map/ppermute | solution.py:13
  804.5 3.2 copy-start.2
  823.9 196.2 %copy-start.15 = (f32[256,1536]{1,0:T(8,128)S(1)}, f32[256,1536]{1,0:T(8,128)}, u32[]{:S(2)}) copy-start(f32[256,1536]{1,0:T(8,128)} %fusion) | copy-start | bytes 4718596
  1021.6 1.2 copy-start.14
  1022.8 7.9 collective-permute-start.32
  1024.7 9.4 collective-permute-start.33
  1027.1 10.8 collective-permute-start.34
  1029.1 12.9 %collective-permute-start.35 = (f32[384,256]{0,1:T(8,128)S(1)}, f32[384,256]{0,1:T(8,128)S(1)}, u32[]{:S(2)}, u32[]{:S(2)}) collective-permute-start(f32[384,256]{0,1:T(8,128)S(1)} %get-tuple-element.16), channel_id=1, source_target_pairs={{1,0},{2,1},{3,2},{4,3},{5,4},{6,5},{7,6},{8,7},{9,8},{10,9},{11,1... | collective-permute-start | bytes 1179656 | tf_op jit(solution)/shard_map/ppermute | solution.py:13
  1063.1 3.2 copy-start.3
  1125.9 3.1 copy-start.17
Sparse Core Ops, SparseCore 0:
  204.0 150.5 all-reduce.4
  811.8 147.1 all-reduce.6
